TPU v7x, 256 devices: a whole 4x4x8 slice. The times are simulated.
256 devices in a mesh: gx: 16 (over x_hi, z), gy: 16 (over x_lo, y, core).
Axes of the slice: x: 4 (x_hi: 2, x_lo: 2; x = x_hi * 2 + x_lo), y: 4, z: 8, core: 2. Of those that a mesh axis runs over, the one named last changes fastest.
Arguments:
- trial_stress: float32 [16, 2048, 2048], P(None, 'gx', 'gy'), may hold values from 1.5 to 3.5
- old_strain: float32 [16, 2048, 2048], P(None, 'gx', 'gy'), may hold values from 0 to 0.5
- yield_mask: int32 [16, 2048, 2048], P(None, 'gx', 'gy'), may hold values from 0 to 1
- newton_count: int32 [16, 2048, 2048], P(None, 'gx', 'gy'), may hold values from 3 to 6
- damage_threshold: float32 [16, 2048, 2048], P(None, 'gx', 'gy'), may hold values from 0.1 to 0.5
Outputs:
- plastic_strain: float32 [16, 2048, 2048], P(None, 'gx', 'gy')
- damage: float32 [16, 2048, 2048], P(None, 'gx', 'gy')
- nodal_force: float32 [2, 16, 2048, 2048], P(None, None, 'gx', 'gy')
All inputs are finite; a program needn't handle non-finite values.
Results may differ from a plain program's by a relative error of at most 0.00002.
Values sent between devices are 32-bit elements; how exact they have to be, the bound alone decides.
A program may use at most 64 MiB of HBM per device.

v0:
```python
import math

import jax
import jax.numpy as jnp
from jax import lax
from jax.sharding import PartitionSpec as P

NEWTON_MAX = 6
OUTER = 3


gauss_taps = [math.exp(-((offset - 8) ** 2) / 32.0) for offset in range(17)]


def extended_2(block, sides, width):
    for axis, dim in sides:
        count = lax.axis_size(axis)
        forward = [(i, i + 1) for i in range(count - 1)]
        backward = [(target, source) for source, target in forward]
        low = lax.ppermute(
            lax.slice_in_dim(block, block.shape[dim] - width, None, axis=dim), axis, forward
        )
        high = lax.ppermute(lax.slice_in_dim(block, 0, width, axis=dim), axis, backward)
        block = jnp.concatenate([low, block, high], axis=dim)
    return block


def from_behind(value, axis, steps):
    count = lax.axis_size(axis)
    first, last = (max(0, -steps), min(count, count - steps))
    return lax.ppermute(value, axis, [(source, source + steps) for source in range(first, last)])


def masked_sweeps(stress_in, strain_in, count_in, damage_in):
    increment = jnp.zeros_like(stress_in)
    soften = 1.0 - 0.5 * damage_in
    for sweep_no in range(1, NEWTON_MAX + 1):
        decay_term = jnp.exp(-4.0 * (strain_in + increment))
        residual = stress_in - increment - (1.0 + 0.5 * (1.0 - decay_term)) * soften
        update = increment + 0.4 * residual / (1.0 + 2.0 * decay_term)
        increment = jnp.where(count_in >= sweep_no, update, increment)
    return increment


def smooth_axis(source, axis_index, length):
    summed = lax.slice_in_dim(source, 0, length, axis=axis_index) * gauss_taps[0]
    for offset in range(1, 17):
        summed = summed + gauss_taps[offset] * lax.slice_in_dim(
            source, offset, offset + length, axis=axis_index
        )
    return summed


def edge_weights(global_start, length, extent):
    positions = global_start + jnp.arange(length, dtype=jnp.int32)
    summed = jnp.zeros((length,), jnp.float32)
    for offset in range(17):
        target = positions + (offset - 8)
        inside = (target >= 0) & (target < extent)
        summed = summed + jnp.where(inside, gauss_taps[offset], 0.0)
    return summed


def local(trial_stress, old_strain, yield_mask, newton_count, damage_threshold):
    layers, row_count, col_count = trial_stress.shape
    counts = yield_mask * newton_count
    weight_z = edge_weights(jnp.int32(0), layers, layers)
    weight_x = edge_weights(
        lax.axis_index("gx") * row_count, row_count, row_count * lax.axis_size("gx")
    )
    weight_y = edge_weights(
        lax.axis_index("gy") * col_count, col_count, col_count * lax.axis_size("gy")
    )
    normal = weight_z[:, None, None] * weight_x[None, :, None] * weight_y[None, None, :]
    damage = jnp.zeros_like(trial_stress)
    for outer_no in range(OUTER):
        increment = masked_sweeps(trial_stress, old_strain, counts, damage)
        plastic_strain = old_strain + increment
        widened = extended_2(plastic_strain, (("gx", 1), ("gy", 2)), 8)
        along_rows = smooth_axis(widened, 1, row_count)
        along_both = smooth_axis(along_rows, 2, col_count)
        depth_padded = jnp.pad(along_both, ((8, 8), (0, 0), (0, 0)))
        averaged = smooth_axis(depth_padded, 0, layers)
        nonlocal_strain = averaged / normal
        damage = 1.0 - jnp.exp(-jnp.maximum(nonlocal_strain - damage_threshold, 0.0) / 0.3)
    stress = (1.0 - damage) * (trial_stress - increment)
    upper_row = from_behind(stress[:, row_count - 1, :], "gx", 1)
    with_upper = jnp.concatenate([upper_row[:, None, :], stress], axis=1)
    left_column = from_behind(with_upper[:, :, col_count - 1], "gy", 1)
    extended = jnp.concatenate([left_column[:, :, None], with_upper], axis=2)
    own_cell = extended[:, 1:, 1:]
    upper_cell = extended[:, :-1, 1:]
    left_cell = extended[:, 1:, :-1]
    corner_cell = extended[:, :-1, :-1]
    force_x = 0.5 * (upper_cell + corner_cell - own_cell - left_cell)
    force_y = 0.5 * (left_cell + corner_cell - own_cell - upper_cell)
    return (plastic_strain, damage, jnp.stack([force_x, force_y]))


def solution(mesh):
    placed = (
        P(None, "gx", "gy"),
        P(None, "gx", "gy"),
        P(None, "gx", "gy"),
        P(None, "gx", "gy"),
        P(None, "gx", "gy"),
    )
    return jax.shard_map(
        local,
        mesh=mesh,
        in_specs=placed,
        out_specs=(P(None, "gx", "gy"), P(None, "gx", "gy"), P(None, None, "gx", "gy")),
        check_vma=False,
    )
```

profile of v0, /device:TPU:6, one launch (start us, length us, event | category | flops | bytes accessed | tf_op | source)
XLA Modules:
  0.0 176.8 jit_solution(8112962999503413900)
XLA Ops:
  0.6 8.8 %fusion.46 = (f32[16,128,128]{2,0,1:T(8,128)S(1)}, pred[16,128,128]{2,0,1:T(8,128)(4,1)S(1)}, pred[16,128,128]{2,0,1:T(8,128)(4,1)}, pred[16,128,128]{2,0,1:T(8,...) fusion(f32[16,128,128]{2,1,0:T(8,128)} %param.6, ...), kind=kLoop, calls=%fused_computation.173 | loop fusion | flops 21757952 | bytes 6815744 | tf_op jit(solution)/shard_map/add | solution.py:78
  9.4 3.8 %collective-permute-start = (f32[16,8,128]{2,0,1:T(8,128)S(1)}, f32[16,8,128]{2,0,1:T(8,128)S(1)}, u32[]{:S(2)}, u32[]{:S(2)}) collective-permute-start(f32[16,8,128]{2,0,1:T(8,128)S(1)} %get-tuple-element.38), channel_id=1, source_target_pairs={{0,16},{16,32},{32,48},{48,64},{64,80},{80,96},{96,112},{112,128},... | collective-permute-start | bytes 196616 | tf_op jit(solution)/shard_map/ppermute | solution.py:20
  13.3 6.7 %collective-permute-start.1 = (f32[16,8,128]{2,0,1:T(8,128)S(1)}, f32[16,8,128]{2,0,1:T(8,128)S(1)}, u32[]{:S(2)}, u32[]{:S(2)}) collective-permute-start(f32[16,8,128]{2,0,1:T(8,128)S(1)} %get-tuple-element.39), channel_id=1, source_target_pairs={{16,0},{32,16},{48,32},{64,48},{80,64},{96,80},{112,96},{128,112},... | collective-permute-start | bytes 196616 | tf_op jit(solution)/shard_map/ppermute | solution.py:23
  20.0 0.1 broadcast_multiply_fusion
  20.1 0.1 collective-permute-done
  20.3 1.6 collective-permute-done.1
  21.8 0.1 pad_maximum_fusion.4
  21.9 1.8 %fusion.259 = (f32[16,144,8]{2,0,1:T(8,128)}, f32[16,144,8]{2,0,1:T(8,128)}) fusion(f32[16,144,128]{2,0,1:T(8,128)S(1)} %pad_maximum_fusion.4), kind=kLoop, calls=%fused_computation.522 | loop fusion | bytes 294912 | tf_op jit(solution)/shard_map/slice | solution.py:21
  23.7 1.9 %copy.168 = f32[16,144,8]{1,2,0:T(8,128)S(1)} copy(f32[16,144,8]{2,0,1:T(8,128)} %get-tuple-element.32) | data formatting | bytes 147456 | tf_op jit(solution)/shard_map/slice | solution.py:21
  25.6 1.9 %collective-permute-start.2 = (f32[16,144,8]{1,2,0:T(8,128)S(1)}, f32[16,144,8]{1,2,0:T(8,128)S(1)}, u32[]{:S(2)}, u32[]{:S(2)}) collective-permute-start(f32[16,144,8]{1,2,0:T(8,128)S(1)} %copy.168), channel_id=1, source_target_pairs={{0,1},{1,2},{2,3},{3,4},{4,5},{5,6},{6,7},{7,8},{8,9},{9,10},{10,1... | collective-permute-start | bytes 221192 | tf_op jit(solution)/shard_map/ppermute | solution.py:20
  27.6 0.6 copy.169
  28.2 5.9 %collective-permute-start.3 = (f32[16,144,8]{1,2,0:T(8,128)S(1)}, f32[16,144,8]{1,2,0:T(8,128)S(1)}, u32[]{:S(2)}, u32[]{:S(2)}) collective-permute-start(f32[16,144,8]{1,2,0:T(8,128)S(1)} %copy.169), channel_id=1, source_target_pairs={{1,0},{2,1},{3,2},{4,3},{5,4},{6,5},{7,6},{8,7},{9,8},{10,9},{11,1... | collective-permute-start | bytes 221192 | tf_op jit(solution)/shard_map/ppermute | solution.py:23
  34.2 0.6 copy.170
  34.7 1.7 collective-permute-done.3
  36.5 1.5 copy.171
  37.9 2.2 %pad_maximum_fusion = f32[16,144,144]{2,0,1:T(8,128)S(1)} fusion(f32[16,144,8]{2,0,1:T(8,128)} %copy.171, f32[16,8,128]{2,0,1:T(8,128)S(1)} %collective-permute-done.1, f32[16,128,128]{2,0,1:T(8,128)S(1)} %get-tuple-element.19, f32[16,8,128]{2,0,1:T(8,128)S(1)} %collective-permute-done, f32[16,144,8]{2,0,1:T(8,128)S(1)} %copy.170), kind=kLoop, calls=%fused_computation.48 | loop fusion | flops 1327104 | bytes 2654208 | tf_op jit(solution)/shard_map/concatenate | solution.py:24
  40.2 4.6 %fusion.30 = f32[16,128,144]{2,0,1:T(8,128)S(1)} fusion(f32[16,144,144]{2,0,1:T(8,128)S(1)} %pad_maximum_fusion), kind=kLoop, calls=%fused_computation.116 | loop fusion | flops 9437184 | bytes 21233664 | tf_op jit(solution)/shard_map/add | solution.py:48
  44.9 4.5 %fusion.192 = f32[16,128,128]{2,0,1:T(8,128)S(1)} fusion(f32[16,128,144]{2,0,1:T(8,128)S(1)} %fusion.30), kind=kLoop, calls=%fused_computation.357 | loop fusion | flops 8388608 | bytes 18874368 | tf_op jit(solution)/shard_map/add | solution.py:48
  49.5 7.3 %fusion.47 = f32[16,128,128]{2,0,1:T(8,128)S(1)} fusion(pred[16,128,128]{2,0,1:T(8,128)(4,1)S(1)} %copy-done.16, pred[16,128,128]{2,0,1:T(8,128)(4,1)S(1)} %copy-done.14, pred[16,128,128]{2,0,1:T(8,128)(4,1)S(1)} %copy-done.12, pred[16,128,128]{2,0,1:T(8,128)(4,1)S(1)} %copy-done.10, pred[16,128,128]{2,0,1:T(8,128)(4,1)S(1)} %copy-done.8, ...), kind=kLoop, calls=%fused_computation.174 | loop fusion | flops 32243712 | bytes 6824448 | tf_op jit(solution)/shard_map/add | solution.py:78
  56.8 1.9 %collective-permute-start.4 = (f32[16,8,128]{2,0,1:T(8,128)S(1)}, f32[16,8,128]{2,0,1:T(8,128)S(1)}, u32[]{:S(2)}, u32[]{:S(2)}) collective-permute-start(f32[16,8,128]{2,0,1:T(8,128)S(1)} %get-tuple-element.36), channel_id=1, source_target_pairs={{0,16},{16,32},{32,48},{48,64},{64,80},{80,96},{96,112},{112,128},... | collective-permute-start | bytes 196616 | tf_op jit(solution)/shard_map/ppermute | solution.py:20
  58.7 7.9 %collective-permute-start.5 = (f32[16,8,128]{2,0,1:T(8,128)S(1)}, f32[16,8,128]{2,0,1:T(8,128)S(1)}, u32[]{:S(2)}, u32[]{:S(2)}) collective-permute-start(f32[16,8,128]{2,0,1:T(8,128)S(1)} %get-tuple-element.37), channel_id=1, source_target_pairs={{16,0},{32,16},{48,32},{64,48},{80,64},{96,80},{112,96},{128,112},... | collective-permute-start | bytes 196616 | tf_op jit(solution)/shard_map/ppermute | solution.py:23
  66.6 0.3 collective-permute-done.4
  66.9 1.6 collective-permute-done.5
  68.5 0.6 copy-done.18
  69.2 1.8 %fusion.258 = (f32[16,144,8]{2,0,1:T(8,128)}, f32[16,144,8]{2,0,1:T(8,128)}) fusion(f32[16,144,128]{2,0,1:T(8,128)S(1)} %pad_maximum_fusion.5), kind=kLoop, calls=%fused_computation.521 | loop fusion | bytes 294912 | tf_op jit(solution)/shard_map/slice | solution.py:21
  71.0 2.5 %copy.185 = f32[16,144,8]{1,2,0:T(8,128)} copy(f32[16,144,8]{2,0,1:T(8,128)} %get-tuple-element.30) | data formatting | bytes 147456 | tf_op jit(solution)/shard_map/slice | solution.py:21
  73.5 1.9 %collective-permute-start.6 = (f32[16,144,8]{1,2,0:T(8,128)}, f32[16,144,8]{1,2,0:T(8,128)}, u32[]{:S(2)}, u32[]{:S(2)}) collective-permute-start(f32[16,144,8]{1,2,0:T(8,128)} %copy.185), channel_id=1, source_target_pairs={{0,1},{1,2},{2,3},{3,4},{4,5},{5,6},{6,7},{7,8},{8,9},{9,10},{10,1... | collective-permute-start | bytes 221192 | tf_op jit(solution)/shard_map/ppermute | solution.py:20
  75.4 2.5 %copy.186 = f32[16,144,8]{1,2,0:T(8,128)} copy(f32[16,144,8]{2,0,1:T(8,128)} %get-tuple-element.31) | data formatting | bytes 147456 | tf_op jit(solution)/shard_map/slice | solution.py:23
  77.9 6.0 %collective-permute-start.7 = (f32[16,144,8]{1,2,0:T(8,128)}, f32[16,144,8]{1,2,0:T(8,128)}, u32[]{:S(2)}, u32[]{:S(2)}) collective-permute-start(f32[16,144,8]{1,2,0:T(8,128)} %copy.186), channel_id=1, source_target_pairs={{1,0},{2,1},{3,2},{4,3},{5,4},{6,5},{7,6},{8,7},{9,8},{10,9},{11,1... | collective-permute-start | bytes 221192 | tf_op jit(solution)/shard_map/ppermute | solution.py:23
  83.9 2.4 %copy.187 = f32[16,144,8]{2,0,1:T(8,128)} copy(f32[16,144,8]{1,2,0:T(8,128)} %collective-permute-done.6) | data formatting | bytes 147456 | tf_op jit(solution)/shard_map/ppermute | solution.py:20
  86.3 0.2 collective-permute-done.7
  86.5 2.4 %copy.188 = f32[16,144,8]{2,0,1:T(8,128)} copy(f32[16,144,8]{1,2,0:T(8,128)} %collective-permute-done.7) | data formatting | bytes 147456 | tf_op jit(solution)/shard_map/ppermute | solution.py:23
  88.9 2.6 %pad_maximum_fusion.1 = f32[16,144,144]{2,0,1:T(8,128)S(1)} fusion(f32[16,144,8]{2,0,1:T(8,128)} %copy.188, f32[16,8,128]{2,0,1:T(8,128)} %copy-done.18, f32[16,128,128]{2,0,1:T(8,128)S(1)} %fusion.47, f32[16,8,128]{2,0,1:T(8,128)S(1)} %collective-permute-done.4, f32[16,144,8]{2,0,1:T(8,128)} %copy.187), kind=kLoop, calls=%fused_computation.49 | loop fusion | flops 1327104 | bytes 2654208 | tf_op jit(solution)/shard_map/concatenate | solution.py:24
  91.5 4.6 %fusion.15 = f32[16,128,144]{2,0,1:T(8,128)S(1)} fusion(f32[16,144,144]{2,0,1:T(8,128)S(1)} %pad_maximum_fusion.1), kind=kLoop, calls=%fused_computation.84 | loop fusion | flops 9437184 | bytes 21233664 | tf_op jit(solution)/shard_map/add | solution.py:48
  96.2 4.5 %fusion.177 = f32[16,128,128]{2,0,1:T(8,128)S(1)} fusion(f32[16,128,144]{2,0,1:T(8,128)S(1)} %fusion.15), kind=kLoop, calls=%fused_computation.325 | loop fusion | flops 8388608 | bytes 18874368 | tf_op jit(solution)/shard_map/add | solution.py:48
  100.7 8.1 %copy_add_fusion = (f32[16,128,128]{2,0,1:T(8,128)S(1)}, f32[16,128,128]{2,0,1:T(8,128)}) fusion(f32[16,128,128]{2,1,0:T(8,128)S(1)} %copy-done.4, pred[16,128,128]{2,0,1:T(8,128)(4,1)S(1)} %copy-done.17, pred[16,128,128]{2,0,1:T(8,128)(4,1)S(1)} %copy-done.15, pred[16,128,128]{2,0,1:T(8,128)(4,1)S(1)} %copy-done.13, ...), kind=kLoop, calls=%fused_computation.395 | loop fusion | flops 32243712 | bytes 7873024 | tf_op jit(solution)/shard_map/add | solution.py:78
  108.8 2.0 %collective-permute-start.8 = (f32[16,8,128]{2,0,1:T(8,128)S(1)}, f32[16,8,128]{2,0,1:T(8,128)S(1)}, u32[]{:S(2)}, u32[]{:S(2)}) collective-permute-start(f32[16,8,128]{2,0,1:T(8,128)S(1)} %get-tuple-element.34), channel_id=1, source_target_pairs={{0,16},{16,32},{32,48},{48,64},{64,80},{80,96},{96,112},{112,128},... | collective-permute-start | bytes 196616 | tf_op jit(solution)/shard_map/ppermute | solution.py:20
  110.8 7.8 %collective-permute-start.9 = (f32[16,8,128]{2,0,1:T(8,128)S(1)}, f32[16,8,128]{2,0,1:T(8,128)S(1)}, u32[]{:S(2)}, u32[]{:S(2)}) collective-permute-start(f32[16,8,128]{2,0,1:T(8,128)S(1)} %get-tuple-element.35), channel_id=1, source_target_pairs={{16,0},{32,16},{48,32},{64,48},{80,64},{96,80},{112,96},{128,112},... | collective-permute-start | bytes 196616 | tf_op jit(solution)/shard_map/ppermute | solution.py:23
  118.6 0.3 collective-permute-done.8
  118.9 1.6 collective-permute-done.9
  120.6 1.8 %fusion.257 = (f32[16,144,8]{2,0,1:T(8,128)}, f32[16,144,8]{2,0,1:T(8,128)}) fusion(f32[16,144,128]{2,0,1:T(8,128)S(1)} %pad_maximum_fusion.6), kind=kLoop, calls=%fused_computation.520 | loop fusion | bytes 294912 | tf_op jit(solution)/shard_map/slice | solution.py:21
  122.4 1.8 %copy.202 = f32[16,144,8]{1,2,0:T(8,128)S(1)} copy(f32[16,144,8]{2,0,1:T(8,128)} %get-tuple-element.28) | data formatting | bytes 147456 | tf_op jit(solution)/shard_map/slice | solution.py:21
  124.2 1.9 %collective-permute-start.10 = (f32[16,144,8]{1,2,0:T(8,128)S(1)}, f32[16,144,8]{1,2,0:T(8,128)S(1)}, u32[]{:S(2)}, u32[]{:S(2)}) collective-permute-start(f32[16,144,8]{1,2,0:T(8,128)S(1)} %copy.202), channel_id=1, source_target_pairs={{0,1},{1,2},{2,3},{3,4},{4,5},{5,6},{6,7},{7,8},{8,9},{9,10},{10,1... | collective-permute-start | bytes 221192 | tf_op jit(solution)/shard_map/ppermute | solution.py:20
  126.1 1.8 %copy.203 = f32[16,144,8]{1,2,0:T(8,128)S(1)} copy(f32[16,144,8]{2,0,1:T(8,128)} %get-tuple-element.29) | data formatting | bytes 147456 | tf_op jit(solution)/shard_map/slice | solution.py:23
  128.0 6.0 %collective-permute-start.11 = (f32[16,144,8]{1,2,0:T(8,128)S(1)}, f32[16,144,8]{1,2,0:T(8,128)S(1)}, u32[]{:S(2)}, u32[]{:S(2)}) collective-permute-start(f32[16,144,8]{1,2,0:T(8,128)S(1)} %copy.203), channel_id=1, source_target_pairs={{1,0},{2,1},{3,2},{4,3},{5,4},{6,5},{7,6},{8,7},{9,8},{10,9},{11,1... | collective-permute-start | bytes 221192 | tf_op jit(solution)/shard_map/ppermute | solution.py:23
  134.0 1.5 copy.204
  135.5 0.7 collective-permute-done.11
  136.2 1.5 copy.205
  137.7 2.6 %pad_maximum_fusion.2 = f32[16,144,144]{2,0,1:T(8,128)S(1)} fusion(f32[16,144,8]{2,0,1:T(8,128)} %copy.205, f32[16,8,128]{2,0,1:T(8,128)S(1)} %collective-permute-done.9, f32[16,128,128]{2,0,1:T(8,128)S(1)} %get-tuple-element.17, f32[16,8,128]{2,0,1:T(8,128)S(1)} %collective-permute-done.8, f32[16,144,8]{2,0,1:T(8,128)} %copy.204), kind=kLoop, calls=%fused_computation.50 | loop fusion | flops 1327104 | bytes 2654208 | tf_op jit(solution)/shard_map/concatenate | solution.py:24
  140.3 4.6 %fusion = f32[16,128,144]{2,0,1:T(8,128)S(1)} fusion(f32[16,144,144]{2,0,1:T(8,128)S(1)} %pad_maximum_fusion.2), kind=kLoop, calls=%fused_computation.52 | loop fusion | flops 9437184 | bytes 21233664 | tf_op jit(solution)/shard_map/add | solution.py:48
  145.0 4.5 %fusion.162 = f32[16,128,128]{2,0,1:T(8,128)S(1)} fusion(f32[16,128,144]{2,0,1:T(8,128)S(1)} %fusion), kind=kLoop, calls=%fused_computation.293 | loop fusion | flops 8388608 | bytes 18874368 | tf_op jit(solution)/shard_map/add | solution.py:48
  149.5 3.9 %subtract_multiply_fusion = (f32[16,128,128]{2,0,1:T(8,128)S(1)}, f32[16,128,128]{2,0,1:T(8,128)}) fusion(f32[16,128,128]{2,0,1:T(8,128)S(1)} %copy-done.6, f32[16,128,128]{2,1,0:T(8,128)S(1)} %copy-done, f32[16,128,128]{2,1,0:T(8,128)S(1)} %copy-done.2, f32[128]{0:T(128)S(1)} %fusion.254, f32[16,128]{0,1:T(8,128)S(1)} %broadcast_multiply_fusion, ...), kind=kLoop, calls=%fused_computation.391 | loop fusion | flops 11010048 | bytes 6300160 | tf_op jit(solution)/shard_map/mul | solution.py:86
  153.4 1.9 %collective-permute-start.12 = (f32[16,128]{1,0:T(8,128)S(1)}, f32[16,128]{1,0:T(8,128)S(1)}, u32[]{:S(2)}, u32[]{:S(2)}) collective-permute-start(f32[16,128]{1,0:T(8,128)S(1)} %slice_bitcast_fusion), channel_id=1, source_target_pairs={{0,16},{16,32},{32,48},{48,64},{64,80},{80,96},{96,112},{112,128},... | collective-permute-start | bytes 24584 | tf_op jit(solution)/shard_map/ppermute | solution.py:31
  155.3 7.6 %collective-permute-done.12 = f32[16,128]{1,0:T(8,128)S(1)} collective-permute-done((f32[16,128]{1,0:T(8,128)S(1)}, f32[16,128]{1,0:T(8,128)S(1)}, u32[]{:S(2)}, u32[]{:S(2)}) %collective-permute-start.12) | collective-permute-done | bytes 8224 | tf_op jit(solution)/shard_map/ppermute | solution.py:31
  162.9 1.3 pad_maximum_fusion.7
  164.2 1.9 %copy.208 = f32[16,129,1]{1,0,2:T(8,128)S(1)} copy(f32[16,129,1]{2,0,1:T(8,128)} %pad_maximum_fusion.7) | data formatting | bytes 16512 | tf_op jit(solution)/shard_map/slice | solution.py:89
  166.2 1.9 %collective-permute-start.13 = (f32[16,129]{1,0:T(8,128)S(1)}, f32[16,129]{1,0:T(8,128)S(1)}, u32[]{:S(2)}, u32[]{:S(2)}) collective-permute-start(f32[16,129]{1,0:T(8,128)S(1)} %bitcast.11), channel_id=1, source_target_pairs={{0,1},{1,2},{2,3},{3,4},{4,5},{5,6},{6,7},{7,8},{8,9},{9,10},{10,1... | collective-permute-start | bytes 24776 | tf_op jit(solution)/shard_map/ppermute | solution.py:31
  168.1 1.3 copy.210
  169.4 1.3 copy.211
  170.7 2.7 %collective-permute-done.13 = f32[16,129]{1,0:T(8,128)S(1)} collective-permute-done((f32[16,129]{1,0:T(8,128)S(1)}, f32[16,129]{1,0:T(8,128)S(1)}, u32[]{:S(2)}, u32[]{:S(2)}) %collective-permute-start.13) | collective-permute-done | bytes 8288 | tf_op jit(solution)/shard_map/ppermute | solution.py:31
  173.3 0.8 copy.209
  174.1 0.6 multiply_bitcast_fusion.1
  174.7 0.1 pad_maximum_fusion.3
  174.9 1.9 %copy.212 = f32[2,16,128,128]{3,2,1,0:T(8,128)} copy(f32[2,16,128,128]{3,1,2,0:T(8,128)S(1)} %pad_maximum_fusion.3) | data formatting | bytes 4194304
  (49 shorter events, 0.4 us)
Async XLA Ops:
  9.4 10.8 %collective-permute-start = (f32[16,8,128]{2,0,1:T(8,128)S(1)}, f32[16,8,128]{2,0,1:T(8,128)S(1)}, u32[]{:S(2)}, u32[]{:S(2)}) collective-permute-start(f32[16,8,128]{2,0,1:T(8,128)S(1)} %get-tuple-element.38), channel_id=1, source_target_pairs={{0,16},{16,32},{32,48},{48,64},{64,80},{80,96},{96,112},{112,128},... | collective-permute-start | bytes 196616 | tf_op jit(solution)/shard_map/ppermute | solution.py:20
  13.3 8.6 %collective-permute-start.1 = (f32[16,8,128]{2,0,1:T(8,128)S(1)}, f32[16,8,128]{2,0,1:T(8,128)S(1)}, u32[]{:S(2)}, u32[]{:S(2)}) collective-permute-start(f32[16,8,128]{2,0,1:T(8,128)S(1)} %get-tuple-element.39), channel_id=1, source_target_pairs={{16,0},{32,16},{48,32},{64,48},{80,64},{96,80},{112,96},{128,112},... | collective-permute-start | bytes 196616 | tf_op jit(solution)/shard_map/ppermute | solution.py:23
  23.7 3.9 %copy-start.5 = (f32[16,144,8]{2,0,1:T(8,128)S(1)}, f32[16,144,8]{2,0,1:T(8,128)}, u32[]{:S(2)}) copy-start(f32[16,144,8]{2,0,1:T(8,128)} %get-tuple-element.33) | copy-start | bytes 221188
  25.6 8.5 %collective-permute-start.2 = (f32[16,144,8]{1,2,0:T(8,128)S(1)}, f32[16,144,8]{1,2,0:T(8,128)S(1)}, u32[]{:S(2)}, u32[]{:S(2)}) collective-permute-start(f32[16,144,8]{1,2,0:T(8,128)S(1)} %copy.168), channel_id=1, source_target_pairs={{0,1},{1,2},{2,3},{3,4},{4,5},{5,6},{6,7},{7,8},{8,9},{9,10},{10,1... | collective-permute-start | bytes 221192 | tf_op jit(solution)/shard_map/ppermute | solution.py:20
  28.2 8.3 %collective-permute-start.3 = (f32[16,144,8]{1,2,0:T(8,128)S(1)}, f32[16,144,8]{1,2,0:T(8,128)S(1)}, u32[]{:S(2)}, u32[]{:S(2)}) collective-permute-start(f32[16,144,8]{1,2,0:T(8,128)S(1)} %copy.169), channel_id=1, source_target_pairs={{1,0},{2,1},{3,2},{4,3},{5,4},{6,5},{7,6},{8,7},{9,8},{10,9},{11,1... | collective-permute-start | bytes 221192 | tf_op jit(solution)/shard_map/ppermute | solution.py:23
  44.8 4.6 %copy-start = (f32[16,128,128]{2,1,0:T(8,128)S(1)}, f32[16,128,128]{2,1,0:T(8,128)}, u32[]{:S(2)}) copy-start(f32[16,128,128]{2,1,0:T(8,128)} %param.5) | copy-start | bytes 3145732
  44.8 4.6 %copy-start.1 = (f32[16,128,128]{2,1,0:T(8,128)S(1)}, f32[16,128,128]{2,1,0:T(8,128)}, u32[]{:S(2)}) copy-start(f32[16,128,128]{2,1,0:T(8,128)} %param.9) | copy-start | bytes 3145732
  44.8 4.6 %copy-start.3 = (f32[16,128,128]{2,1,0:T(8,128)S(1)}, f32[16,128,128]{2,1,0:T(8,128)}, u32[]{:S(2)}) copy-start(f32[16,128,128]{2,1,0:T(8,128)} %param.6) | copy-start | bytes 3145732
  44.8 4.6 %copy-start.8 = (pred[16,128,128]{2,0,1:T(8,128)(4,1)S(1)}, pred[16,128,128]{2,0,1:T(8,128)(4,1)}, u32[]{:S(2)}) copy-start(pred[16,128,128]{2,0,1:T(8,128)(4,1)} %get-tuple-element.21) | copy-start | bytes 786436
  44.8 4.6 %copy-start.10 = (pred[16,128,128]{2,0,1:T(8,128)(4,1)S(1)}, pred[16,128,128]{2,0,1:T(8,128)(4,1)}, u32[]{:S(2)}) copy-start(pred[16,128,128]{2,0,1:T(8,128)(4,1)} %get-tuple-element.22) | copy-start | bytes 786436
  44.8 4.6 %copy-start.12 = (pred[16,128,128]{2,0,1:T(8,128)(4,1)S(1)}, pred[16,128,128]{2,0,1:T(8,128)(4,1)}, u32[]{:S(2)}) copy-start(pred[16,128,128]{2,0,1:T(8,128)(4,1)} %get-tuple-element.23) | copy-start | bytes 786436
  44.9 4.6 %copy-start.14 = (pred[16,128,128]{2,0,1:T(8,128)(4,1)S(1)}, pred[16,128,128]{2,0,1:T(8,128)(4,1)}, u32[]{:S(2)}) copy-start(pred[16,128,128]{2,0,1:T(8,128)(4,1)} %get-tuple-element.24) | copy-start | bytes 786436
  44.9 4.6 %copy-start.16 = (pred[16,128,128]{2,0,1:T(8,128)(4,1)S(1)}, pred[16,128,128]{2,0,1:T(8,128)(4,1)}, u32[]{:S(2)}) copy-start(pred[16,128,128]{2,0,1:T(8,128)(4,1)} %get-tuple-element.25) | copy-start | bytes 786436
  56.8 10.1 %collective-permute-start.4 = (f32[16,8,128]{2,0,1:T(8,128)S(1)}, f32[16,8,128]{2,0,1:T(8,128)S(1)}, u32[]{:S(2)}, u32[]{:S(2)}) collective-permute-start(f32[16,8,128]{2,0,1:T(8,128)S(1)} %get-tuple-element.36), channel_id=1, source_target_pairs={{0,16},{16,32},{32,48},{48,64},{64,80},{80,96},{96,112},{112,128},... | collective-permute-start | bytes 196616 | tf_op jit(solution)/shard_map/ppermute | solution.py:20
  58.7 9.8 %collective-permute-start.5 = (f32[16,8,128]{2,0,1:T(8,128)S(1)}, f32[16,8,128]{2,0,1:T(8,128)S(1)}, u32[]{:S(2)}, u32[]{:S(2)}) collective-permute-start(f32[16,8,128]{2,0,1:T(8,128)S(1)} %get-tuple-element.37), channel_id=1, source_target_pairs={{16,0},{32,16},{48,32},{64,48},{80,64},{96,80},{112,96},{128,112},... | collective-permute-start | bytes 196616 | tf_op jit(solution)/shard_map/ppermute | solution.py:23
  68.5 0.6 copy-start.18
  73.5 10.4 %collective-permute-start.6 = (f32[16,144,8]{1,2,0:T(8,128)}, f32[16,144,8]{1,2,0:T(8,128)}, u32[]{:S(2)}, u32[]{:S(2)}) collective-permute-start(f32[16,144,8]{1,2,0:T(8,128)} %copy.185), channel_id=1, source_target_pairs={{0,1},{1,2},{2,3},{3,4},{4,5},{5,6},{6,7},{7,8},{8,9},{9,10},{10,1... | collective-permute-start | bytes 221192 | tf_op jit(solution)/shard_map/ppermute | solution.py:20
  77.9 8.6 %collective-permute-start.7 = (f32[16,144,8]{1,2,0:T(8,128)}, f32[16,144,8]{1,2,0:T(8,128)}, u32[]{:S(2)}, u32[]{:S(2)}) collective-permute-start(f32[16,144,8]{1,2,0:T(8,128)} %copy.186), channel_id=1, source_target_pairs={{1,0},{2,1},{3,2},{4,3},{5,4},{6,5},{7,6},{8,7},{9,8},{10,9},{11,1... | collective-permute-start | bytes 221192 | tf_op jit(solution)/shard_map/ppermute | solution.py:23
  96.1 4.6 %copy-start.4 = (f32[16,128,128]{2,1,0:T(8,128)S(1)}, f32[16,128,128]{2,1,0:T(8,128)}, u32[]{:S(2)}) copy-start(f32[16,128,128]{2,1,0:T(8,128)} %param.6) | copy-start | bytes 3145732
  96.1 4.6 %copy-start.9 = (pred[16,128,128]{2,0,1:T(8,128)(4,1)S(1)}, pred[16,128,128]{2,0,1:T(8,128)(4,1)}, u32[]{:S(2)}) copy-start(pred[16,128,128]{2,0,1:T(8,128)(4,1)} %get-tuple-element.21) | copy-start | bytes 786436
  96.1 4.6 %copy-start.11 = (pred[16,128,128]{2,0,1:T(8,128)(4,1)S(1)}, pred[16,128,128]{2,0,1:T(8,128)(4,1)}, u32[]{:S(2)}) copy-start(pred[16,128,128]{2,0,1:T(8,128)(4,1)} %get-tuple-element.22) | copy-start | bytes 786436
  96.2 4.6 %copy-start.13 = (pred[16,128,128]{2,0,1:T(8,128)(4,1)S(1)}, pred[16,128,128]{2,0,1:T(8,128)(4,1)}, u32[]{:S(2)}) copy-start(pred[16,128,128]{2,0,1:T(8,128)(4,1)} %get-tuple-element.23) | copy-start | bytes 786436
  96.2 4.6 %copy-start.15 = (pred[16,128,128]{2,0,1:T(8,128)(4,1)S(1)}, pred[16,128,128]{2,0,1:T(8,128)(4,1)}, u32[]{:S(2)}) copy-start(pred[16,128,128]{2,0,1:T(8,128)(4,1)} %get-tuple-element.24) | copy-start | bytes 786436
  96.2 4.6 %copy-start.17 = (pred[16,128,128]{2,0,1:T(8,128)(4,1)S(1)}, pred[16,128,128]{2,0,1:T(8,128)(4,1)}, u32[]{:S(2)}) copy-start(pred[16,128,128]{2,0,1:T(8,128)(4,1)} %get-tuple-element.25) | copy-start | bytes 786436
  108.8 10.1 %collective-permute-start.8 = (f32[16,8,128]{2,0,1:T(8,128)S(1)}, f32[16,8,128]{2,0,1:T(8,128)S(1)}, u32[]{:S(2)}, u32[]{:S(2)}) collective-permute-start(f32[16,8,128]{2,0,1:T(8,128)S(1)} %get-tuple-element.34), channel_id=1, source_target_pairs={{0,16},{16,32},{32,48},{48,64},{64,80},{80,96},{96,112},{112,128},... | collective-permute-start | bytes 196616 | tf_op jit(solution)/shard_map/ppermute | solution.py:20
  110.8 9.7 %collective-permute-start.9 = (f32[16,8,128]{2,0,1:T(8,128)S(1)}, f32[16,8,128]{2,0,1:T(8,128)S(1)}, u32[]{:S(2)}, u32[]{:S(2)}) collective-permute-start(f32[16,8,128]{2,0,1:T(8,128)S(1)} %get-tuple-element.35), channel_id=1, source_target_pairs={{16,0},{32,16},{48,32},{64,48},{80,64},{96,80},{112,96},{128,112},... | collective-permute-start | bytes 196616 | tf_op jit(solution)/shard_map/ppermute | solution.py:23
  124.2 9.8 %collective-permute-start.10 = (f32[16,144,8]{1,2,0:T(8,128)S(1)}, f32[16,144,8]{1,2,0:T(8,128)S(1)}, u32[]{:S(2)}, u32[]{:S(2)}) collective-permute-start(f32[16,144,8]{1,2,0:T(8,128)S(1)} %copy.202), channel_id=1, source_target_pairs={{0,1},{1,2},{2,3},{3,4},{4,5},{5,6},{6,7},{7,8},{8,9},{9,10},{10,1... | collective-permute-start | bytes 221192 | tf_op jit(solution)/shard_map/ppermute | solution.py:20
  128.0 8.3 %collective-permute-start.11 = (f32[16,144,8]{1,2,0:T(8,128)S(1)}, f32[16,144,8]{1,2,0:T(8,128)S(1)}, u32[]{:S(2)}, u32[]{:S(2)}) collective-permute-start(f32[16,144,8]{1,2,0:T(8,128)S(1)} %copy.203), channel_id=1, source_target_pairs={{1,0},{2,1},{3,2},{4,3},{5,4},{6,5},{7,6},{8,7},{9,8},{10,9},{11,1... | collective-permute-start | bytes 221192 | tf_op jit(solution)/shard_map/ppermute | solution.py:23
  144.9 4.5 %copy-start.2 = (f32[16,128,128]{2,1,0:T(8,128)S(1)}, f32[16,128,128]{2,1,0:T(8,128)}, u32[]{:S(2)}) copy-start(f32[16,128,128]{2,1,0:T(8,128)} %param.9) | copy-start | bytes 3145732
  144.9 4.5 %copy-start.6 = (f32[16,128,128]{2,0,1:T(8,128)S(1)}, f32[16,128,128]{2,0,1:T(8,128)}, u32[]{:S(2)}) copy-start(f32[16,128,128]{2,0,1:T(8,128)} %get-tuple-element.18) | copy-start | bytes 3145732
  153.4 9.5 %collective-permute-start.12 = (f32[16,128]{1,0:T(8,128)S(1)}, f32[16,128]{1,0:T(8,128)S(1)}, u32[]{:S(2)}, u32[]{:S(2)}) collective-permute-start(f32[16,128]{1,0:T(8,128)S(1)} %slice_bitcast_fusion), channel_id=1, source_target_pairs={{0,16},{16,32},{32,48},{48,64},{64,80},{80,96},{96,112},{112,128},... | collective-permute-start | bytes 24584 | tf_op jit(solution)/shard_map/ppermute | solution.py:31
  164.2 5.2 %copy-start.7 = (f32[16,128,128]{2,0,1:T(8,128)S(1)}, f32[16,128,128]{2,0,1:T(8,128)}, u32[]{:S(2)}) copy-start(f32[16,128,128]{2,0,1:T(8,128)} %get-tuple-element.16) | copy-start | bytes 3145732
  166.2 7.2 %collective-permute-start.13 = (f32[16,129]{1,0:T(8,128)S(1)}, f32[16,129]{1,0:T(8,128)S(1)}, u32[]{:S(2)}, u32[]{:S(2)}) collective-permute-start(f32[16,129]{1,0:T(8,128)S(1)} %bitcast.11), channel_id=1, source_target_pairs={{0,1},{1,2},{2,3},{3,4},{4,5},{5,6},{6,7},{7,8},{8,9},{9,10},{10,1... | collective-permute-start | bytes 24776 | tf_op jit(solution)/shard_map/ppermute | solution.py:31
where the time goes:
time: 178 us; the launch traced here: 177 us
  other arithmetic  65.2 us (37%)
  starting transfers between devices  57.7 us (32%)
  local copies, waits for them, and re-layouts  34.4 us (19%)
  waiting for transfers between devices  18.3 us (10%)
    ppermute x6, starting transfers between devices, extended_2(): lax.ppermute(lax.slice_in_dim(block, 0, width, axis=dim), axis, backward)  40.3 us
    add x6, other arithmetic, smooth_axis(): summed + gauss_taps[offset] * lax.slice_in_dim(source, offset, offset + l...  27.2 us
    add x3, other arithmetic, local(): plastic_strain = old_strain + increment  24.2 us
    ppermute x6, starting transfers between devices, extended_2(): lax.ppermute(lax.slice_in_dim(block, block.shape[dim] - width, None, axis...  13.5 us
    slice x9, local copies, waits for them, and re-layouts, extended_2(): lax.slice_in_dim(block, block.shape[dim] - width, None, axis=dim)  11.6 us
    ppermute x2, waiting for transfers between devices, from_behind(): lax.ppermute(value, axis, [(source, source + steps) for source in range(f...  10.2 us
    concatenate x6, other arithmetic, extended_2(): block = jnp.concatenate([low, block, high], axis=dim)  7.7 us
    ppermute x6, waiting for transfers between devices, extended_2(): lax.ppermute(lax.slice_in_dim(block, 0, width, axis=dim), axis, backward)  7.36 us
  transfers between devices with their start and end apart: 14, of which 11 were waited for; matrix products, arithmetic and copies ran while one was open for 7% of the time, Pallas kernels for 0%

commit v1 on v0

v1 whole, which is shorter than its diff:
```python
import functools
import math

import jax
import jax.numpy as jnp
import numpy as np
from jax import lax
from jax.experimental import pallas as pl
from jax.experimental.pallas import tpu as pltpu
from jax.sharding import PartitionSpec as P

NEWTON_MAX = 6
OUTER = 3
CZ = 16
B = 128
R = 8
ROWS = 16
BLOCKS = B // ROWS
LOG2E = 1.0 / math.log(2.0)
KAPPA = 4.0 * LOG2E
LOG5 = math.log2(5.0)
F32 = jnp.float32
BF16 = jnp.bfloat16
MESH = pl.DeviceIdType.MESH


def tap(t):
    t = np.asarray(t, np.float64)
    return np.where(np.abs(t) <= R, np.exp(-t * t / 32.0), 0.0)


def two(m):
    hi = np.asarray(m, np.float64).astype(BF16)
    lo = (m - hi.astype(np.float64)).astype(BF16)
    return hi, lo


def axis_norm(first, last, n):
    at = np.arange(n)
    norm = np.zeros(n)
    for off in range(-R, R + 1):
        to = at + off
        inside = np.ones(n, bool)
        if first:
            inside &= to >= 0
        if last:
            inside &= to < n
        norm += np.where(inside, tap(off), 0.0)
    return norm


def axis_matrix(first, last):
    out = np.arange(B)[:, None]
    col = np.arange(B + 2 * R)[None, :] - R
    return tap(out - col) / axis_norm(first, last, B)[:, None]


def depth_matrix():
    at = np.arange(CZ)
    return tap(at[:, None] - at[None, :]) / axis_norm(True, True, CZ)[:, None]


def tables():
    wy, wx, ae = [], [], []
    for first, last in ((True, False), (False, False), (False, True)):
        ext = axis_matrix(first, last)
        own = ext[:, R : R + B]
        hi, lo = two(own.T)
        wy.append(np.block([[hi, lo], [hi, lo]]))
        hi, lo = two(own)
        wx.append(np.block([[hi, hi], [lo, lo]]))
        wide = np.zeros((B, 2 * B))
        wide[:, : B + 2 * R] = ext
        ae.append(np.concatenate(two(wide), axis=0))
    az = depth_matrix()
    full = np.exp(-(np.arange(-R, R + 1) ** 2) / 32.0).sum()
    by = np.zeros((2 * B, 2 * B))
    bx = np.zeros((2 * B, 2 * B))
    for z in range(CZ):
        for j in range(R):
            lane = 16 * (z % 8) + 8 * (z // 8) + j
            for zo in range(CZ):
                base = 128 * (zo // 8) + 16 * (zo % 8)
                for r in range(R):
                    by[lane, base + 8 + r] = az[zo, z] * tap(r - (j - 8)) / full
                    by[B + lane, base + r] = az[zo, z] * tap(r - 8 - j) / full
                    bx[8 * zo + r, 8 * z + j] = az[zo, z] * tap(r - (j - 8)) / full
                    bx[B + 8 * zo + r, B + 8 * z + j] = az[zo, z] * tap(r - 8 - j) / full
    return (
        np.stack(wy),
        np.stack(wx),
        np.stack(ae),
        np.stack(two(by)),
        np.concatenate(two(bx), axis=0),
    )


def split(v):
    hi = v.astype(BF16)
    return hi, (v - hi.astype(F32)).astype(BF16)


def dot(a, b):
    return jnp.dot(a, b, preferred_element_type=F32)


def recip(v):
    r = pltpu.reciprocal(v, approx=True)
    return r * (2.0 - v * r)


def newton(start, goal, beta, count):
    y = start
    for s in range(1, NEWTON_MAX + 1):
        part = y * recip(jnp.exp2(y - goal) + 2.5)
        moved = (y - beta) - part
        y = moved if s <= 3 else jnp.where(count >= s, moved, y)
    return (goal - y) * (1.0 / KAPPA) + LOG5 / KAPPA


def depth_halves():
    az = depth_matrix()
    return 0.5 * (az[:8, :8] + az[:8, :7:-1]), 0.5 * (az[:8, :8] - az[:8, :7:-1])


def smooth_depth(planes):
    even, odd = depth_halves()
    add = [planes[z] + planes[CZ - 1 - z] for z in range(8)]
    sub = [planes[z] - planes[CZ - 1 - z] for z in range(8)]
    out = [None] * CZ
    for z in range(8):
        e = float(even[z, 0]) * add[0]
        o = float(odd[z, 0]) * sub[0]
        for i in range(1, 8):
            e = e + float(even[z, i]) * add[i]
            o = o + float(odd[z, i]) * sub[i]
        out[z] = e + o
        out[CZ - 1 - z] = e - o
    return out


KERNEL_VMEM = 30 << 20
FORCE_VMEM = 12 << 20
CHUNKS = ((0, 16), (112, 16), (16, 48), (64, 48))


def kernel(
    nx, ny,
    t_h, old_h, mask_h, cnt_h, thr_h, wy_h, wx_h, ae_h, by_h, bx_h,
    p_o, d_o, se, frec,
    t_v, old_v, mask_v, cnt_v, thr_v, g_v, p_s, zhl, t2, nl, hout, yhi, ylo, pack, hrec, xrec,
    wy, wx, ae, by, bx, fpack,
    in_sem, w_sem, send, recv,
):
    gx = lax.axis_index("gx")
    gy = lax.axis_index("gy")
    p_v = [p_s.at[0], p_s.at[1], p_o]
    up, dn, lf, rt = gx > 0, gx < nx - 1, gy > 0, gy < ny - 1

    def variant(i, n):
        return jnp.where(i == 0, 0, jnp.where(i == n - 1, 2, 1))

    ins = ((t_h, t_v), (old_h, old_v), (mask_h, mask_v), (cnt_h, cnt_v), (thr_h, thr_v))
    loads = []
    for c, (r0, n) in enumerate(CHUNKS):
        for a, (src, dst) in enumerate(ins[:4]):
            copy = pltpu.make_async_copy(src.at[:, r0 : r0 + n, :], dst.at[:, r0 : r0 + n, :], in_sem.at[c, a])
            copy.start()
            loads.append(copy)
    weights = [
        pltpu.make_async_copy(wy_h.at[variant(gy, ny)], wy, w_sem.at[0]),
        pltpu.make_async_copy(wx_h.at[variant(gx, nx)], wx, w_sem.at[1]),
        pltpu.make_async_copy(ae_h.at[variant(gx, nx)], ae, w_sem.at[2]),
        pltpu.make_async_copy(by_h, by, w_sem.at[3]),
        pltpu.make_async_copy(bx_h, bx, w_sem.at[4]),
        pltpu.make_async_copy(thr_h, thr_v, w_sem.at[5]),
    ]
    for copy in weights:
        copy.start()

    barrier = pltpu.get_barrier_semaphore()
    for dx in (-1, 0, 1):
        for dy in (-1, 0, 1):
            if dx == 0 and dy == 0:
                continue
            here = [c for c, on in ((up, dx < 0), (dn, dx > 0), (lf, dy < 0), (rt, dy > 0)) if on]

            @pl.when(functools.reduce(jnp.logical_and, here))
            def _(dx=dx, dy=dy):
                pl.semaphore_signal(barrier, inc=1, device_id=(gx + dx, gy + dy), device_id_type=MESH)

    one = jnp.int32(1)
    zero = jnp.int32(0)
    across = jnp.where(up, one, zero) + jnp.where(dn, one, zero) + 1
    along = jnp.where(lf, one, zero) + jnp.where(rt, one, zero) + 1
    pl.semaphore_wait(barrier, across * along - 1)

    @pl.when(jnp.logical_not(up))
    def _():
        for k in range(OUTER):
            xrec[k, 0] = jnp.zeros((CZ, R, B), F32)
            hrec[k, :, 0:R, :] = jnp.zeros((2, R, B), F32)
        se[:, 0:R, :] = jnp.zeros((CZ, R, B), F32)
        frec[0:R, :] = jnp.zeros((R, B), F32)

    @pl.when(jnp.logical_not(dn))
    def _():
        for k in range(OUTER):
            xrec[k, 1] = jnp.zeros((CZ, R, B), F32)
            hrec[k, :, R + B :, :] = jnp.zeros((2, R, B), F32)

    @pl.when(jnp.logical_not(lf))
    def _():
        for k in range(OUTER):
            hrec[k, 0] = jnp.zeros((B + 2 * R, B), F32)
        frec[...] = jnp.zeros((B + R, B), F32)

    @pl.when(jnp.logical_not(rt))
    def _():
        for k in range(OUTER):
            hrec[k, 1] = jnp.zeros((B + 2 * R, B), F32)

    yhi[...] = jnp.zeros_like(yhi)
    ylo[...] = jnp.zeros_like(ylo)

    lane = lax.broadcasted_iota(jnp.int32, (ROWS, B), 1)
    slot = lane // 16
    low = (lane % 16) < 8
    rim = jnp.logical_or(lane < R, lane >= B - R)

    def rdma(k, i, src, dst, dx, dy):
        ix = jnp.clip(gx + dx, 0, nx - 1)
        iy = jnp.clip(gy + dy, 0, ny - 1)
        return pltpu.make_async_remote_copy(
            src_ref=src, dst_ref=dst, send_sem=send.at[k, i], recv_sem=recv.at[k, i],
            device_id=(ix, iy), device_id_type=MESH,
        )

    def faces(k):
        both = jnp.logical_and
        top, bottom = slice(0, R), slice(B - R, B)
        after = slice(R + B, 2 * R + B)
        return [
            (up, dn, rdma(k, 0, p_v[k].at[:, top, :], xrec.at[k, 1], -1, 0)),
            (dn, up, rdma(k, 1, p_v[k].at[:, bottom, :], xrec.at[k, 0], 1, 0)),
            (both(dn, rt), both(up, lf), rdma(k, 2, pack.at[k, 1, bottom], hrec.at[k, 0, top], 1, 1)),
            (both(up, rt), both(dn, lf), rdma(k, 3, pack.at[k, 1, top], hrec.at[k, 0, after], -1, 1)),
            (both(dn, lf), both(up, rt), rdma(k, 4, pack.at[k, 0, bottom], hrec.at[k, 1, top], 1, -1)),
            (both(up, lf), both(dn, rt), rdma(k, 5, pack.at[k, 0, top], hrec.at[k, 1, after], -1, -1)),
        ]

    def sides(k, c):
        r0, n = CHUNKS[c]
        here, there = slice(r0, r0 + n), slice(R + r0, R + r0 + n)
        return [
            (rt, lf, rdma(k, 6 + 2 * c, pack.at[k, 1, here], hrec.at[k, 0, there], 0, 1)),
            (lf, rt, rdma(k, 7 + 2 * c, pack.at[k, 0, here], hrec.at[k, 1, there], 0, -1)),
        ]

    def start(copies):
        for sends, _, copy in copies:
            pl.when(sends)(copy.start)

    def finish(copies):
        for sends, gets, copy in copies:
            pl.when(gets)(copy.wait_recv)
            pl.when(sends)(copy.wait_send)

    def block_of(i):
        return jnp.where(i == 0, 0, jnp.where(i == 1, BLOCKS - 1, i - 1))

    def rows_of(i):
        return pl.ds(pl.multiple_of(block_of(i) * ROWS, ROWS), ROWS)

    def halo_add(z, at):
        h, zz = z // 8, z % 8
        part = pltpu.roll(hout[at, 128 * h : 128 * h + 128], (120 - 16 * zz) % 128, 1)
        return nl[z, at, :] + jnp.where(rim, part, 0.0)

    def damage_left(z, at):
        over = jnp.maximum(halo_add(z, at) - thr_v[z, at, :], 0.0)
        return jnp.exp2(over * (-LOG2E / 0.3))

    def update(k, i):
        at = rows_of(i)
        for z in range(CZ):
            if k == 0:
                t, old = t_v[z, at, :], old_v[z, at, :]
                count = mask_v[z, at, :] * cnt_v[z, at, :]
                cnt_v[z, at, :] = count
                g0 = KAPPA * (t + old) - LOG5
                y0 = KAPPA * t
                g_v[z, at, :] = g0
                t_v[z, at, :] = y0
                beta = 0.1 * KAPPA
                p = newton(y0 - 17.5 * beta, g0 - 17.5 * beta, beta, count)
            else:
                old = old_v[z, at, :]
                count = cnt_v[z, at, :]
                beta = (0.05 * KAPPA) * damage_left(z, at) + 0.05 * KAPPA
                reach = 17.5 * beta
                p = newton(t_v[z, at, :] - reach, g_v[z, at, :] - reach, beta, count)
            p_v[k][z, at, :] = jnp.where(count > 0, p, old)
        halves = []
        for h in range(2):
            acc = None
            for zz in range(8):
                turned = pltpu.roll(p_v[k][8 * h + zz, at, :], (16 * zz + 8) % 128, 1)
                acc = turned if acc is None else jnp.where(slot == zz, turned, acc)
            halves.append(acc)
        a, b = halves
        pack[k, 1, at, :] = jnp.where(low, a, pltpu.roll(b, 8, 1))
        pack[k, 0, at, :] = jnp.where(low, pltpu.roll(a, 120, 1), b)
        for r in range(0, ROWS, 8):
            at8 = pl.ds(pl.multiple_of(block_of(i) * ROWS + r, 8), 8)
            for z, plane in enumerate(smooth_depth([p_v[k][z, at8, :] for z in range(CZ)])):
                zhl[z, r : r + 8, :] = plane
        hi, lo = split(zhl[...].reshape(CZ * ROWS, B))
        t = dot(jnp.concatenate([hi, lo], axis=1), wy[...])
        hi, lo = split(t[:, :B] + t[:, B:])
        below = pl.ds(pl.multiple_of(block_of(i) * ROWS + B, ROWS), ROWS)
        for z in range(CZ):
            half, rows = pl.ds(128 * (z % 2), 128), slice(ROWS * z, ROWS * z + ROWS)
            t2[z // 2, at, half] = hi[rows]
            t2[z // 2, below, half] = lo[rows]

    def sweep_all(k):
        def body(i, carry):
            if k == 0:
                for c in range(4):
                    @pl.when(i == (0, 1, 2, 5)[c])
                    def _(c=c):
                        for copy in loads[4 * c : 4 * c + 4]:
                            copy.wait()
                @pl.when(i == 0)
                def _():
                    for copy in weights:
                        copy.wait()

            update(k, i)

            @pl.when(i == 1)
            def _():
                start(faces(k))
                start(sides(k, 0))
                start(sides(k, 1))

            @pl.when(i == 4)
            def _():
                start(sides(k, 2))

            return carry

        lax.fori_loop(0, BLOCKS, body, 0)
        start(sides(k, 3))

    def own_rows():
        def body(i, carry):
            o = dot(wx[...], t2[i])
            o = o[:B] + o[B:]
            nl[2 * i] = o[:, :B]
            nl[2 * i + 1] = o[:, B:]
            return carry

        lax.fori_loop(0, CZ // 2, body, 0)

    def halos(k):
        finish(faces(k))
        for c in range(4):
            finish(sides(k, c))
        hi, lo = split(jnp.concatenate([hrec[k, 0], hrec[k, 1]], axis=1))
        yh = dot(hi, by[0]) + dot(lo, by[0]) + dot(hi, by[1])
        hi, lo = split(yh)
        yhi[0 : B + 2 * R, :] = hi
        ylo[0 : B + 2 * R, :] = lo
        both = dot(ae[...], yhi[...])
        hout[...] = both[:B] + both[B:] + dot(ae[:B, :], ylo[...])
        hi, lo = split(xrec[k].reshape(2 * B, B))
        g = dot(jnp.concatenate([hi, lo], axis=1), wy[...])
        hi, lo = split(g[:, :B] + g[:, B:])
        o = dot(bx[...], jnp.concatenate([hi, lo], axis=1))
        o = o[: 2 * B, :B] + o[: 2 * B, B:] + o[2 * B :, :B]
        o = o.reshape(2, CZ, R, B)
        nl[:, 0:R, :] += o[0]
        nl[:, B - R :, :] += o[1]

    for k in range(OUTER):
        sweep_all(k)
        own_rows()
        halos(k)

    def last(i, carry):
        at = rows_of(i)
        acc = jnp.zeros((ROWS, B), F32)
        inside = pl.ds(pl.multiple_of(block_of(i) * ROWS + R, R), ROWS)
        for z in range(CZ):
            left = damage_left(z, at)
            d_o[z, at, :] = 1.0 - left
            stress = left * ((g_v[z, at, :] + LOG5) * (1.0 / KAPPA) - p_o[z, at, :])
            se[z, inside, :] = stress
            acc = jnp.where(lane == z, pltpu.roll(stress, (z + 1) % 128, 1), acc)
        fpack[at, :] = acc
        return carry

    lax.fori_loop(0, BLOCKS, last, 0)
    both = jnp.logical_and
    ends = [
        (rt, lf, rdma(OUTER, 0, fpack, frec.at[R:, :], 0, 1)),
        (dn, up, rdma(OUTER, 1, se.at[:, B + R - 1 : B + R, :], se.at[:, R - 1 : R, :], 1, 0)),
        (both(dn, rt), both(up, lf), rdma(OUTER, 2, fpack.at[B - R :, :], frec.at[:R, :], 1, 1)),
    ]
    start(ends)
    finish(ends)


def forces(se, frec, p_v, d_v, p_h, d_h, f_h, f_v, sem):
    copies = [pltpu.make_async_copy(p_v, p_h, sem.at[0]), pltpu.make_async_copy(d_v, d_h, sem.at[1])]
    for copy in copies:
        copy.start()
    lane8 = lax.broadcasted_iota(jnp.int32, (R, B), 1)
    row8 = lax.broadcasted_iota(jnp.int32, (R, B), 0)

    for z in range(CZ):
        above = left = None
        for i in range(B // R + 1):
            at8 = slice(R * i, R * i + R)
            s = se[z, at8, :]
            col = frec[at8, :]
            if z:
                col = pltpu.roll(col, 128 - z, 1)
            l = jnp.where(lane8 == 0, col, pltpu.roll(s, 1, 1))
            if i:
                s_up = pltpu.roll(jnp.where(row8 == R - 1, above, s), 1, 0)
                l_up = pltpu.roll(jnp.where(row8 == R - 1, left, l), 1, 0)
                a = 0.5 * (l_up - s)
                b = 0.5 * (s_up - l)
                f_v[0, z, R * i - R : R * i, :] = a + b
                f_v[1, z, R * i - R : R * i, :] = a - b
            above, left = s, l
        for c in range(2):
            copies.append(pltpu.make_async_copy(f_v.at[c, z], f_h.at[c, z], sem.at[2 + 2 * z + c]))
            copies[-1].start()
    for copy in copies:
        copy.wait()


def solution(mesh):
    nx, ny = mesh.shape["gx"], mesh.shape["gy"]
    consts = tables()
    hbm = pl.BlockSpec(memory_space=pltpu.MemorySpace.HBM)
    vmem = pl.BlockSpec(memory_space=pltpu.MemorySpace.VMEM)
    block = jax.ShapeDtypeStruct((CZ, B, B), F32)
    scratch = [
        pltpu.VMEM((CZ, B, B), F32),
        pltpu.VMEM((CZ, B, B), F32),
        pltpu.VMEM((CZ, B, B), jnp.int32),
        pltpu.VMEM((CZ, B, B), jnp.int32),
        pltpu.VMEM((CZ, B, B), F32),
        pltpu.VMEM((CZ, B, B), F32),
        pltpu.VMEM((OUTER - 1, CZ, B, B), F32),
        pltpu.VMEM((CZ, ROWS, B), F32),
        pltpu.VMEM((CZ // 2, 2 * B, 2 * B), BF16),
        pltpu.VMEM((CZ, B, B), F32),
        pltpu.VMEM((B, 2 * B), F32),
        pltpu.VMEM((2 * B, 2 * B), BF16),
        pltpu.VMEM((2 * B, 2 * B), BF16),
        pltpu.VMEM((OUTER, 2, B, B), F32),
        pltpu.VMEM((OUTER, 2, B + 2 * R, B), F32),
        pltpu.VMEM((OUTER, 2, CZ, R, B), F32),
        pltpu.VMEM((2 * B, 2 * B), BF16),
        pltpu.VMEM((2 * B, 2 * B), BF16),
        pltpu.VMEM((2 * B, 2 * B), BF16),
        pltpu.VMEM((2, 2 * B, 2 * B), BF16),
        pltpu.VMEM((4 * B, 2 * B), BF16),
        pltpu.VMEM((B, B), F32),
        pltpu.SemaphoreType.DMA((4, 4)),
        pltpu.SemaphoreType.DMA((6,)),
        pltpu.SemaphoreType.DMA((OUTER + 1, 14)),
        pltpu.SemaphoreType.DMA((OUTER + 1, 14)),
    ]

    def local(*args):
        p, d, stress, column = pl.pallas_call(
            functools.partial(kernel, nx, ny),
            out_shape=(
                block,
                block,
                jax.ShapeDtypeStruct((CZ, B + R, B), F32),
                jax.ShapeDtypeStruct((B + R, B), F32),
            ),
            in_specs=[hbm] * 10,
            out_specs=[vmem] * 4,
            scratch_shapes=scratch,
            compiler_params=pltpu.CompilerParams(
                collective_id=0, has_side_effects=True, vmem_limit_bytes=KERNEL_VMEM
            ),
        )(*[pltpu.with_memory_space_constraint(a, pltpu.MemorySpace.HBM) for a in (*args, *[jnp.asarray(c) for c in consts])])
        return pl.pallas_call(
            forces,
            out_shape=(block, block, jax.ShapeDtypeStruct((2, CZ, B, B), F32)),
            in_specs=[vmem] * 4,
            out_specs=[hbm] * 3,
            scratch_shapes=[pltpu.VMEM((2, CZ, B, B), F32), pltpu.SemaphoreType.DMA((2 + 2 * CZ,))],
            compiler_params=pltpu.CompilerParams(vmem_limit_bytes=FORCE_VMEM),
        )(stress, column, p, d)

    placed = P(None, "gx", "gy")
    return jax.shard_map(
        local,
        mesh=mesh,
        in_specs=(placed,) * 5,
        out_specs=(placed, placed, P(None, None, "gx", "gy")),
        check_vma=False,
    )
```

time: 178 us -> 47.8 us (0.27)
  other arithmetic: 65.2 us -> 0 us
  starting transfers between devices: 57.7 us -> 0 us
  Pallas kernels: 0 us -> 46.8 us
  local copies, waits for them, and re-layouts: 34.4 us -> 0 us
  waiting for transfers between devices: 18.3 us -> 0 us
    ppermute x14 -> x0, starting transfers between devices: 57.7 us -> none  [the longest x6 40.3 us: extended_2(): lax.ppermute(lax.slice_in_dim(block, 0, width, axis=dim), axis, backward)]
    add x12 -> x0, other arithmetic: 51.5 us -> none  [the longest x6 27.2 us: smooth_axis(): summed + gauss_taps[offset] * lax.slice_in_dim(source, offset, offset + l...]
    pallas_call x0 -> x2, Pallas kernels: none -> 46.8 us  [the longest x1 44.5 us: local(): pl.pallas_call(functools.partial(kernel, nx, ny), out_shape=(block, block...]
    slice x13 -> x0, local copies, waits for them, and re-layouts: 18.5 us -> none  [the longest x9 11.6 us: extended_2(): lax.slice_in_dim(block, block.shape[dim] - width, None, axis=dim)]
    ppermute x14 -> x0, waiting for transfers between devices: 18.3 us -> none  [the longest x2 10.2 us: from_behind(): lax.ppermute(value, axis, [(source, source + steps) for source in range(f...]
    ppermute x6 -> x0, local copies, waits for them, and re-layouts: 9.84 us -> none  [the longest x3 5.37 us: extended_2(): lax.ppermute(lax.slice_in_dim(block, 0, width, axis=dim), axis, backward)]
    concatenate x7 -> x0, other arithmetic: 9.01 us -> none  [the longest x6 7.7 us: extended_2(): block = jnp.concatenate([low, block, high], axis=dim)]
    unnamed x41 -> x0, local copies, waits for them, and re-layouts: 5.25 us -> none
  transfers between devices with their start and end apart: 14 -> 0, of which waited for: 11 -> 0; matrix products, arithmetic and copies ran while one was open for 7% -> 0% of each run, Pallas kernels for 0% -> 0%
where the time goes in v1:
time: 47.8 us; the launch traced here: 47.4 us
  Pallas kernels  46.8 us (98%)
  between operations  0.64 us (1%)
    pallas_call x1, Pallas kernels, local(): pl.pallas_call(functools.partial(kernel, nx, ny), out_shape=(block, block...  44.5 us
    pallas_call x1, Pallas kernels, local(): pl.pallas_call(forces, out_shape=(block, block, jax.ShapeDtypeStruct((2,...  2.28 us

profile of v1, /device:TPU:6, one launch (start us, length us, event | category | flops | bytes accessed | tf_op | source)
XLA Modules:
  0.0 47.4 jit_solution(6952051058469034438)
XLA Ops:
  0.6 44.5 %shard_map.121 = (f32[16,128,128]{2,1,0:T(8,128)S(1)}, f32[16,128,128]{2,1,0:T(8,128)S(1)}, f32[16,136,128]{2,1,0:T(8,128)S(1)}, f32[136,128]{1,0:T(8,128)S(1)}) custom-call(f32[16,128,128]{2,1,0:T(8,128)} %t_h.1, f32[16,128,128]{2,1,0:T(8,128)} %old_h.1, s32[16,128,128]{2,1,0:T(8,128)} %mask_h.1, s32[16,128,128]{2,1,0:T(8,128)} %cnt_h.1, ...), custom_call_target="tpu_custom_call" | custom-call | tf_op jit(solution)/shard_map/pallas_call | solution.py:483
  45.1 2.3 %shard_map.122 = (f32[16,128,128]{2,1,0:T(8,128)}, f32[16,128,128]{2,1,0:T(8,128)}, f32[2,16,128,128]{3,2,1,0:T(8,128)}) custom-call(f32[16,136,128]{2,1,0:T(8,128)S(1)} %get-tuple-element.7.se, f32[136,128]{1,0:T(8,128)S(1)} %get-tuple-element.8.frec, f32[16,128,128]{2,1,0:T(8,128)S(1)} %get-tuple-element.9.p_v, f32[16,128,128]{2,1,0:T(8,128)S(1)} %get-tuple-element.10.d_v), custom_call_target="tpu_custom_call" | custom-call | tf_op jit(solution)/shard_map/pallas_call | solution.py:498
